TPU v7x, 256 devices: a whole 4x4x8 slice. The times are simulated.
256 devices in a mesh: row: 32 (over z, x_lo, core), col: 8 (over y, x_hi).
Axes of the slice: x: 4 (x_hi: 2, x_lo: 2; x = x_hi * 2 + x_lo), y: 4, z: 8, core: 2. Of those that a mesh axis runs over, the one named last changes fastest.
Arguments:
- activations: bfloat16 [512, 8192], P('col', 'row'), may hold values from -6 to 6
- cotangent: bfloat16 [512, 14336], P('row', 'col'), may hold values from -0.109375 to 0.109375
- accumulated: bfloat16 [8192, 14336], P('row', 'col'), may hold values from -3 to 3
- band_old: float32 [8192, 16, 256], P('row', 'col'), may hold values from -6 to 6
- diagonal_old: float32 [8192, 256], P(('row', 'col')), may hold values from -6 to 6
Outputs:
- band_new: float32 [8192, 16, 256], P('row', 'col')
- diagonal_new: float32 [8192, 256], P(('row', 'col'))
All inputs are finite; a program needn't handle non-finite values.
Results may differ from a plain program's by a relative error of at most 0.0018.
Values may be sent and summed in bfloat16 or wider, within the bound.
A program may use at most 64 MiB of HBM per device.

v0:
```python
import jax
import jax.numpy as jnp
from jax import lax
from jax.sharding import PartitionSpec as P

decay_rate = 0.95


def from_behind(shard, axis, by):
    count = lax.axis_size(axis)
    return lax.ppermute(shard, axis, [(i, (i + by) % count) for i in range(count)])


def gradient_tile(columns, cotangent_all, accumulated):
    product = lax.dot_general(
        columns, cotangent_all, (((0,), (0,)), ((), ())), preferred_element_type=jnp.float32
    )
    return (product + accumulated.astype(jnp.float32)).astype(jnp.bfloat16)


def block_product(left, right):
    return lax.dot_general(
        left, right, (((1,), (1,)), ((), ())), preferred_element_type=jnp.float32
    )


def store_block(partials, gram_block, offset):
    start = jnp.asarray(offset, jnp.int32) - 1
    anchor_index = jnp.zeros((), jnp.int32)
    return lax.dynamic_update_slice(
        partials, gram_block[:, None, :], (anchor_index, start, anchor_index)
    )


def body(activations, cotangent, accumulated, band_old, diagonal_old):
    columns = lax.all_gather(activations, "col", axis=0, tiled=True)
    cotangent_all = lax.all_gather(cotangent, "row", axis=0, tiled=True)
    own_panel = gradient_tile(columns, cotangent_all, accumulated)
    block_rows = own_panel.shape[0]
    band_count = lax.axis_size("row") // 2
    diagonal_part = block_product(own_panel, own_panel)
    partials = jnp.zeros((block_rows, band_count, block_rows), jnp.float32)

    def cycle_step(offset, loop_state):
        moving, partials = loop_state
        moving = from_behind(moving, "row", 1)
        partials = store_block(partials, block_product(own_panel, moving), offset)
        return (moving, partials)

    moving, partials = lax.fori_loop(1, band_count + 1, cycle_step, (own_panel, partials))
    summed_band, summed_diagonal = lax.psum((partials, diagonal_part), "col")
    position = lax.axis_index("col")
    share_width = band_count // lax.axis_size("col")
    share_rows = block_rows // lax.axis_size("col")
    band_sum = lax.dynamic_slice_in_dim(summed_band, position * share_width, share_width, 1)
    diagonal_sum = lax.dynamic_slice_in_dim(summed_diagonal, position * share_rows, share_rows, 0)
    band_new = decay_rate * band_old + (1.0 - decay_rate) * band_sum
    diagonal_new = decay_rate * diagonal_old + (1.0 - decay_rate) * diagonal_sum
    return (band_new, diagonal_new)


def solution(mesh):
    in_specs = (
        P("col", "row"),
        P("row", "col"),
        P("row", "col"),
        P("row", "col", None),
        P(("row", "col"), None),
    )
    out_specs = (P("row", "col", None), P(("row", "col"), None))
    return jax.shard_map(body, mesh=mesh, in_specs=in_specs, out_specs=out_specs, check_vma=False)
```

profile of v0, /device:TPU:1, one launch (start us, length us, event | category | flops | bytes accessed | tf_op | source)
XLA Modules:
  0.0 655.8 jit_solution(671231376424157284)
XLA Ops:
  8.0 30.6 %all_gather.6 = bf16[512,256]{1,0:T(8,128)(2,1)S(1)} all-gather(bf16[64,256]{1,0:T(8,128)(2,1)} %param.7), channel_id=1, replica_groups=mesh['row'=32,'col'=8] {'col'}, dimensions={0}, use_global_device_ids=true | all-gather | bytes 294912 | tf_op jit(solution)/shard_map/all_gather | solution.py:36
  38.5 39.7 %all-gather.2.cloned.1.call-done = bf16[512,1792]{1,0:T(8,128)(2,1)} async-done(((bf16[16,1792]{1,0:T(8,128)(2,1)}), bf16[512,1792]{1,0:T(8,128)(2,1)}) %all-gather.2.cloned.1.call-update) | async-done | bytes 1835024 | tf_op jit(solution)/shard_map/all_gather | solution.py:37
  81.8 351.5 %while.19 = (s32[]{:T(128)}, bf16[256,1792]{1,0:T(8,128)(2,1)S(1)}, f32[256,16,256]{2,1,0:T(8,128)}, bf16[256,1792]{1,0:T(8,128)(2,1)S(1)}, s32[]{:T(128)}, /*index=5*/s32[]{:T(128)}) while((s32[]{:T(128)}, bf16[256,1792]{1,0:T(8,128)(2,1)S(1)}, f32[256,16,256]{2,1,0:T(8,128)}, bf16[256,1792]{1,0:T(8,128)(2,1)S(1)}, s32[]{:T(128)}, ...), condition=%wide.region_1.0_spmd, body=%wide.region_0.0_spmd.sunk | while | flops 234881024 | bytes 8650873 | solution.py:50
  82.6 10.3 %collective-permute-done = bf16[256,1792]{1,0:T(8,128)(2,1)S(1)} collective-permute-done((bf16[256,1792]{1,0:T(8,128)(2,1)S(1)}, bf16[256,1792]{1,0:T(8,128)(2,1)S(1)}, u32[]{:S(2)}, u32[]{:S(2)}) %collective-permute-start) | collective-permute-done | bytes 917536 | tf_op jit(solution)/shard_map/while/body/eval_jaxpr/ppermute | solution.py:11
  103.2 10.3 %collective-permute-done = bf16[256,1792]{1,0:T(8,128)(2,1)S(1)} collective-permute-done((bf16[256,1792]{1,0:T(8,128)(2,1)S(1)}, bf16[256,1792]{1,0:T(8,128)(2,1)S(1)}, u32[]{:S(2)}, u32[]{:S(2)}) %collective-permute-start) | collective-permute-done | bytes 917536 | tf_op jit(solution)/shard_map/while/body/eval_jaxpr/ppermute | solution.py:11
  123.9 10.3 %collective-permute-done = bf16[256,1792]{1,0:T(8,128)(2,1)S(1)} collective-permute-done((bf16[256,1792]{1,0:T(8,128)(2,1)S(1)}, bf16[256,1792]{1,0:T(8,128)(2,1)S(1)}, u32[]{:S(2)}, u32[]{:S(2)}) %collective-permute-start) | collective-permute-done | bytes 917536 | tf_op jit(solution)/shard_map/while/body/eval_jaxpr/ppermute | solution.py:11
  144.5 10.3 %collective-permute-done = bf16[256,1792]{1,0:T(8,128)(2,1)S(1)} collective-permute-done((bf16[256,1792]{1,0:T(8,128)(2,1)S(1)}, bf16[256,1792]{1,0:T(8,128)(2,1)S(1)}, u32[]{:S(2)}, u32[]{:S(2)}) %collective-permute-start) | collective-permute-done | bytes 917536 | tf_op jit(solution)/shard_map/while/body/eval_jaxpr/ppermute | solution.py:11
  165.1 10.3 %collective-permute-done = bf16[256,1792]{1,0:T(8,128)(2,1)S(1)} collective-permute-done((bf16[256,1792]{1,0:T(8,128)(2,1)S(1)}, bf16[256,1792]{1,0:T(8,128)(2,1)S(1)}, u32[]{:S(2)}, u32[]{:S(2)}) %collective-permute-start) | collective-permute-done | bytes 917536 | tf_op jit(solution)/shard_map/while/body/eval_jaxpr/ppermute | solution.py:11
  185.8 12.1 %collective-permute-done = bf16[256,1792]{1,0:T(8,128)(2,1)S(1)} collective-permute-done((bf16[256,1792]{1,0:T(8,128)(2,1)S(1)}, bf16[256,1792]{1,0:T(8,128)(2,1)S(1)}, u32[]{:S(2)}, u32[]{:S(2)}) %collective-permute-start) | collective-permute-done | bytes 917536 | tf_op jit(solution)/shard_map/while/body/eval_jaxpr/ppermute | solution.py:11
  206.4 14.2 %collective-permute-done = bf16[256,1792]{1,0:T(8,128)(2,1)S(1)} collective-permute-done((bf16[256,1792]{1,0:T(8,128)(2,1)S(1)}, bf16[256,1792]{1,0:T(8,128)(2,1)S(1)}, u32[]{:S(2)}, u32[]{:S(2)}) %collective-permute-start) | collective-permute-done | bytes 917536 | tf_op jit(solution)/shard_map/while/body/eval_jaxpr/ppermute | solution.py:11
  228.4 14.9 %collective-permute-done = bf16[256,1792]{1,0:T(8,128)(2,1)S(1)} collective-permute-done((bf16[256,1792]{1,0:T(8,128)(2,1)S(1)}, bf16[256,1792]{1,0:T(8,128)(2,1)S(1)}, u32[]{:S(2)}, u32[]{:S(2)}) %collective-permute-start) | collective-permute-done | bytes 917536 | tf_op jit(solution)/shard_map/while/body/eval_jaxpr/ppermute | solution.py:11
  251.1 14.9 %collective-permute-done = bf16[256,1792]{1,0:T(8,128)(2,1)S(1)} collective-permute-done((bf16[256,1792]{1,0:T(8,128)(2,1)S(1)}, bf16[256,1792]{1,0:T(8,128)(2,1)S(1)}, u32[]{:S(2)}, u32[]{:S(2)}) %collective-permute-start) | collective-permute-done | bytes 917536 | tf_op jit(solution)/shard_map/while/body/eval_jaxpr/ppermute | solution.py:11
  266.8 7.0 %dynamic_update_slice.14 = f32[256,16,256]{2,1,0:T(8,128)} dynamic-update-slice(f32[256,16,256]{2,1,0:T(8,128)} %get-tuple-element.187, f32[256,1,256]{2,1,0:T(1,128)S(1)} %copy.11, s32[]{:T(128)} %constant.65.clone.1..sunk, s32[]{:T(128)S(6)} %copy.16, s32[]{:T(128)} %constant.65.clone.1..sunk) | dynamic-update-slice | bytes 524292 | tf_op jit(solution)/shard_map/while/body/eval_jaxpr/dynamic_update_slice | solution.py:30
  273.9 14.9 %collective-permute-done = bf16[256,1792]{1,0:T(8,128)(2,1)S(1)} collective-permute-done((bf16[256,1792]{1,0:T(8,128)(2,1)S(1)}, bf16[256,1792]{1,0:T(8,128)(2,1)S(1)}, u32[]{:S(2)}, u32[]{:S(2)}) %collective-permute-start) | collective-permute-done | bytes 917536 | tf_op jit(solution)/shard_map/while/body/eval_jaxpr/ppermute | solution.py:11
  296.7 14.9 %collective-permute-done = bf16[256,1792]{1,0:T(8,128)(2,1)S(1)} collective-permute-done((bf16[256,1792]{1,0:T(8,128)(2,1)S(1)}, bf16[256,1792]{1,0:T(8,128)(2,1)S(1)}, u32[]{:S(2)}, u32[]{:S(2)}) %collective-permute-start) | collective-permute-done | bytes 917536 | tf_op jit(solution)/shard_map/while/body/eval_jaxpr/ppermute | solution.py:11
  319.5 14.9 %collective-permute-done = bf16[256,1792]{1,0:T(8,128)(2,1)S(1)} collective-permute-done((bf16[256,1792]{1,0:T(8,128)(2,1)S(1)}, bf16[256,1792]{1,0:T(8,128)(2,1)S(1)}, u32[]{:S(2)}, u32[]{:S(2)}) %collective-permute-start) | collective-permute-done | bytes 917536 | tf_op jit(solution)/shard_map/while/body/eval_jaxpr/ppermute | solution.py:11
  342.3 14.9 %collective-permute-done = bf16[256,1792]{1,0:T(8,128)(2,1)S(1)} collective-permute-done((bf16[256,1792]{1,0:T(8,128)(2,1)S(1)}, bf16[256,1792]{1,0:T(8,128)(2,1)S(1)}, u32[]{:S(2)}, u32[]{:S(2)}) %collective-permute-start) | collective-permute-done | bytes 917536 | tf_op jit(solution)/shard_map/while/body/eval_jaxpr/ppermute | solution.py:11
  357.9 7.0 %dynamic_update_slice.14 = f32[256,16,256]{2,1,0:T(8,128)} dynamic-update-slice(f32[256,16,256]{2,1,0:T(8,128)} %get-tuple-element.187, f32[256,1,256]{2,1,0:T(1,128)S(1)} %copy.11, s32[]{:T(128)} %constant.65.clone.1..sunk, s32[]{:T(128)S(6)} %copy.16, s32[]{:T(128)} %constant.65.clone.1..sunk) | dynamic-update-slice | bytes 524292 | tf_op jit(solution)/shard_map/while/body/eval_jaxpr/dynamic_update_slice | solution.py:30
  365.1 14.9 %collective-permute-done = bf16[256,1792]{1,0:T(8,128)(2,1)S(1)} collective-permute-done((bf16[256,1792]{1,0:T(8,128)(2,1)S(1)}, bf16[256,1792]{1,0:T(8,128)(2,1)S(1)}, u32[]{:S(2)}, u32[]{:S(2)}) %collective-permute-start) | collective-permute-done | bytes 917536 | tf_op jit(solution)/shard_map/while/body/eval_jaxpr/ppermute | solution.py:11
  380.7 7.0 %dynamic_update_slice.14 = f32[256,16,256]{2,1,0:T(8,128)} dynamic-update-slice(f32[256,16,256]{2,1,0:T(8,128)} %get-tuple-element.187, f32[256,1,256]{2,1,0:T(1,128)S(1)} %copy.11, s32[]{:T(128)} %constant.65.clone.1..sunk, s32[]{:T(128)S(6)} %copy.16, s32[]{:T(128)} %constant.65.clone.1..sunk) | dynamic-update-slice | bytes 524292 | tf_op jit(solution)/shard_map/while/body/eval_jaxpr/dynamic_update_slice | solution.py:30
  387.8 14.9 %collective-permute-done = bf16[256,1792]{1,0:T(8,128)(2,1)S(1)} collective-permute-done((bf16[256,1792]{1,0:T(8,128)(2,1)S(1)}, bf16[256,1792]{1,0:T(8,128)(2,1)S(1)}, u32[]{:S(2)}, u32[]{:S(2)}) %collective-permute-start) | collective-permute-done | bytes 917536 | tf_op jit(solution)/shard_map/while/body/eval_jaxpr/ppermute | solution.py:11
  403.5 7.0 %dynamic_update_slice.14 = f32[256,16,256]{2,1,0:T(8,128)} dynamic-update-slice(f32[256,16,256]{2,1,0:T(8,128)} %get-tuple-element.187, f32[256,1,256]{2,1,0:T(1,128)S(1)} %copy.11, s32[]{:T(128)} %constant.65.clone.1..sunk, s32[]{:T(128)S(6)} %copy.16, s32[]{:T(128)} %constant.65.clone.1..sunk) | dynamic-update-slice | bytes 524292 | tf_op jit(solution)/shard_map/while/body/eval_jaxpr/dynamic_update_slice | solution.py:30
  410.6 14.9 %collective-permute-done = bf16[256,1792]{1,0:T(8,128)(2,1)S(1)} collective-permute-done((bf16[256,1792]{1,0:T(8,128)(2,1)S(1)}, bf16[256,1792]{1,0:T(8,128)(2,1)S(1)}, u32[]{:S(2)}, u32[]{:S(2)}) %collective-permute-start) | collective-permute-done | bytes 917536 | tf_op jit(solution)/shard_map/while/body/eval_jaxpr/ppermute | solution.py:11
  433.4 211.4 %all-reduce.3.cloned.1.call-done = (f32[256,16,256]{2,1,0:T(8,128)}, f32[256,256]{1,0:T(8,128)}) async-done(((f32[256,16,256]{2,1,0:T(8,128)}, f32[256,256]{1,0:T(8,128)}), (f32[256,16,256]{2,1,0:T(8,128)}, f32[256,256]{1,0:T(8,128)})) %all-reduce.3.cloned.1.call-update) | async-done | bytes 4456464 | tf_op jit(solution)/shard_map/psum | solution.py:51
  (90 shorter events, 119.4 us)
Async XLA Ops:
  7.2 71.1 %all-gather.2.cloned.1.call-start = ((), (), s32[]{:S(2)}) async-start(), calls=%async_computation | async-start | bytes 1892352 | tf_op jit(solution)/shard_map/all_gather | solution.py:37
  7.9 636.9 %all-reduce.3.cloned.1.call-start = ((), (), s32[]{:S(2)}) async-start(), calls=%async_computation.1 | async-start | bytes 8912896 | tf_op jit(solution)/shard_map/psum | solution.py:51
  81.8 11.1 %collective-permute-start = (bf16[256,1792]{1,0:T(8,128)(2,1)S(1)}, bf16[256,1792]{1,0:T(8,128)(2,1)S(1)}, u32[]{:S(2)}, u32[]{:S(2)}) collective-permute-start(bf16[256,1792]{1,0:T(8,128)(2,1)S(1)} %get-tuple-element.186), channel_id=1, source_target_pairs={{0,8},{8,16},{16,24},{24,32},{32,40},{40,48},{48,56},{56,64},{64,7... | collective-permute-start | bytes 2752520 | tf_op jit(solution)/shard_map/while/body/eval_jaxpr/ppermute | solution.py:11
  100.7 12.9 %collective-permute-start = (bf16[256,1792]{1,0:T(8,128)(2,1)S(1)}, bf16[256,1792]{1,0:T(8,128)(2,1)S(1)}, u32[]{:S(2)}, u32[]{:S(2)}) collective-permute-start(bf16[256,1792]{1,0:T(8,128)(2,1)S(1)} %get-tuple-element.186), channel_id=1, source_target_pairs={{0,8},{8,16},{16,24},{24,32},{32,40},{40,48},{48,56},{56,64},{64,7... | collective-permute-start | bytes 2752520 | tf_op jit(solution)/shard_map/while/body/eval_jaxpr/ppermute | solution.py:11
  121.3 12.9 %collective-permute-start = (bf16[256,1792]{1,0:T(8,128)(2,1)S(1)}, bf16[256,1792]{1,0:T(8,128)(2,1)S(1)}, u32[]{:S(2)}, u32[]{:S(2)}) collective-permute-start(bf16[256,1792]{1,0:T(8,128)(2,1)S(1)} %get-tuple-element.186), channel_id=1, source_target_pairs={{0,8},{8,16},{16,24},{24,32},{32,40},{40,48},{48,56},{56,64},{64,7... | collective-permute-start | bytes 2752520 | tf_op jit(solution)/shard_map/while/body/eval_jaxpr/ppermute | solution.py:11
  141.9 12.9 %collective-permute-start = (bf16[256,1792]{1,0:T(8,128)(2,1)S(1)}, bf16[256,1792]{1,0:T(8,128)(2,1)S(1)}, u32[]{:S(2)}, u32[]{:S(2)}) collective-permute-start(bf16[256,1792]{1,0:T(8,128)(2,1)S(1)} %get-tuple-element.186), channel_id=1, source_target_pairs={{0,8},{8,16},{16,24},{24,32},{32,40},{40,48},{48,56},{56,64},{64,7... | collective-permute-start | bytes 2752520 | tf_op jit(solution)/shard_map/while/body/eval_jaxpr/ppermute | solution.py:11
  162.6 12.9 %collective-permute-start = (bf16[256,1792]{1,0:T(8,128)(2,1)S(1)}, bf16[256,1792]{1,0:T(8,128)(2,1)S(1)}, u32[]{:S(2)}, u32[]{:S(2)}) collective-permute-start(bf16[256,1792]{1,0:T(8,128)(2,1)S(1)} %get-tuple-element.186), channel_id=1, source_target_pairs={{0,8},{8,16},{16,24},{24,32},{32,40},{40,48},{48,56},{56,64},{64,7... | collective-permute-start | bytes 2752520 | tf_op jit(solution)/shard_map/while/body/eval_jaxpr/ppermute | solution.py:11
  183.2 14.6 %collective-permute-start = (bf16[256,1792]{1,0:T(8,128)(2,1)S(1)}, bf16[256,1792]{1,0:T(8,128)(2,1)S(1)}, u32[]{:S(2)}, u32[]{:S(2)}) collective-permute-start(bf16[256,1792]{1,0:T(8,128)(2,1)S(1)} %get-tuple-element.186), channel_id=1, source_target_pairs={{0,8},{8,16},{16,24},{24,32},{32,40},{40,48},{48,56},{56,64},{64,7... | collective-permute-start | bytes 2752520 | tf_op jit(solution)/shard_map/while/body/eval_jaxpr/ppermute | solution.py:11
  205.5 15.0 %collective-permute-start = (bf16[256,1792]{1,0:T(8,128)(2,1)S(1)}, bf16[256,1792]{1,0:T(8,128)(2,1)S(1)}, u32[]{:S(2)}, u32[]{:S(2)}) collective-permute-start(bf16[256,1792]{1,0:T(8,128)(2,1)S(1)} %get-tuple-element.186), channel_id=1, source_target_pairs={{0,8},{8,16},{16,24},{24,32},{32,40},{40,48},{48,56},{56,64},{64,7... | collective-permute-start | bytes 2752520 | tf_op jit(solution)/shard_map/while/body/eval_jaxpr/ppermute | solution.py:11
  228.3 15.0 %collective-permute-start = (bf16[256,1792]{1,0:T(8,128)(2,1)S(1)}, bf16[256,1792]{1,0:T(8,128)(2,1)S(1)}, u32[]{:S(2)}, u32[]{:S(2)}) collective-permute-start(bf16[256,1792]{1,0:T(8,128)(2,1)S(1)} %get-tuple-element.186), channel_id=1, source_target_pairs={{0,8},{8,16},{16,24},{24,32},{32,40},{40,48},{48,56},{56,64},{64,7... | collective-permute-start | bytes 2752520 | tf_op jit(solution)/shard_map/while/body/eval_jaxpr/ppermute | solution.py:11
  251.0 15.0 %collective-permute-start = (bf16[256,1792]{1,0:T(8,128)(2,1)S(1)}, bf16[256,1792]{1,0:T(8,128)(2,1)S(1)}, u32[]{:S(2)}, u32[]{:S(2)}) collective-permute-start(bf16[256,1792]{1,0:T(8,128)(2,1)S(1)} %get-tuple-element.186), channel_id=1, source_target_pairs={{0,8},{8,16},{16,24},{24,32},{32,40},{40,48},{48,56},{56,64},{64,7... | collective-permute-start | bytes 2752520 | tf_op jit(solution)/shard_map/while/body/eval_jaxpr/ppermute | solution.py:11
  273.8 15.0 %collective-permute-start = (bf16[256,1792]{1,0:T(8,128)(2,1)S(1)}, bf16[256,1792]{1,0:T(8,128)(2,1)S(1)}, u32[]{:S(2)}, u32[]{:S(2)}) collective-permute-start(bf16[256,1792]{1,0:T(8,128)(2,1)S(1)} %get-tuple-element.186), channel_id=1, source_target_pairs={{0,8},{8,16},{16,24},{24,32},{32,40},{40,48},{48,56},{56,64},{64,7... | collective-permute-start | bytes 2752520 | tf_op jit(solution)/shard_map/while/body/eval_jaxpr/ppermute | solution.py:11
  296.6 15.0 %collective-permute-start = (bf16[256,1792]{1,0:T(8,128)(2,1)S(1)}, bf16[256,1792]{1,0:T(8,128)(2,1)S(1)}, u32[]{:S(2)}, u32[]{:S(2)}) collective-permute-start(bf16[256,1792]{1,0:T(8,128)(2,1)S(1)} %get-tuple-element.186), channel_id=1, source_target_pairs={{0,8},{8,16},{16,24},{24,32},{32,40},{40,48},{48,56},{56,64},{64,7... | collective-permute-start | bytes 2752520 | tf_op jit(solution)/shard_map/while/body/eval_jaxpr/ppermute | solution.py:11
  319.4 15.0 %collective-permute-start = (bf16[256,1792]{1,0:T(8,128)(2,1)S(1)}, bf16[256,1792]{1,0:T(8,128)(2,1)S(1)}, u32[]{:S(2)}, u32[]{:S(2)}) collective-permute-start(bf16[256,1792]{1,0:T(8,128)(2,1)S(1)} %get-tuple-element.186), channel_id=1, source_target_pairs={{0,8},{8,16},{16,24},{24,32},{32,40},{40,48},{48,56},{56,64},{64,7... | collective-permute-start | bytes 2752520 | tf_op jit(solution)/shard_map/while/body/eval_jaxpr/ppermute | solution.py:11
  342.2 15.0 %collective-permute-start = (bf16[256,1792]{1,0:T(8,128)(2,1)S(1)}, bf16[256,1792]{1,0:T(8,128)(2,1)S(1)}, u32[]{:S(2)}, u32[]{:S(2)}) collective-permute-start(bf16[256,1792]{1,0:T(8,128)(2,1)S(1)} %get-tuple-element.186), channel_id=1, source_target_pairs={{0,8},{8,16},{16,24},{24,32},{32,40},{40,48},{48,56},{56,64},{64,7... | collective-permute-start | bytes 2752520 | tf_op jit(solution)/shard_map/while/body/eval_jaxpr/ppermute | solution.py:11
  365.0 15.0 %collective-permute-start = (bf16[256,1792]{1,0:T(8,128)(2,1)S(1)}, bf16[256,1792]{1,0:T(8,128)(2,1)S(1)}, u32[]{:S(2)}, u32[]{:S(2)}) collective-permute-start(bf16[256,1792]{1,0:T(8,128)(2,1)S(1)} %get-tuple-element.186), channel_id=1, source_target_pairs={{0,8},{8,16},{16,24},{24,32},{32,40},{40,48},{48,56},{56,64},{64,7... | collective-permute-start | bytes 2752520 | tf_op jit(solution)/shard_map/while/body/eval_jaxpr/ppermute | solution.py:11
  387.7 15.0 %collective-permute-start = (bf16[256,1792]{1,0:T(8,128)(2,1)S(1)}, bf16[256,1792]{1,0:T(8,128)(2,1)S(1)}, u32[]{:S(2)}, u32[]{:S(2)}) collective-permute-start(bf16[256,1792]{1,0:T(8,128)(2,1)S(1)} %get-tuple-element.186), channel_id=1, source_target_pairs={{0,8},{8,16},{16,24},{24,32},{32,40},{40,48},{48,56},{56,64},{64,7... | collective-permute-start | bytes 2752520 | tf_op jit(solution)/shard_map/while/body/eval_jaxpr/ppermute | solution.py:11
  410.5 15.0 %collective-permute-start = (bf16[256,1792]{1,0:T(8,128)(2,1)S(1)}, bf16[256,1792]{1,0:T(8,128)(2,1)S(1)}, u32[]{:S(2)}, u32[]{:S(2)}) collective-permute-start(bf16[256,1792]{1,0:T(8,128)(2,1)S(1)} %get-tuple-element.186), channel_id=1, source_target_pairs={{0,8},{8,16},{16,24},{24,32},{32,40},{40,48},{48,56},{56,64},{64,7... | collective-permute-start | bytes 2752520 | tf_op jit(solution)/shard_map/while/body/eval_jaxpr/ppermute | solution.py:11
  433.3 211.5 %copy-start = (f32[256,2,256]{2,1,0:T(2,128)S(1)}, f32[256,2,256]{2,1,0:T(2,128)}, u32[]{:S(2)}) copy-start(f32[256,2,256]{2,1,0:T(2,128)} %param.10) | copy-start | bytes 1572868
  433.3 214.3 %copy-start.1 = (f32[32,256]{1,0:T(8,128)S(1)}, f32[32,256]{1,0:T(8,128)}, u32[]{:S(2)}) copy-start(f32[32,256]{1,0:T(8,128)} %param.11) | copy-start | bytes 98308
Sparse Core Ops, SparseCore 0:
  9.8 68.3 all-gather.1
  433.5 211.2 all-reduce.2
where the time goes:
time: 658 us; the launch traced here: 656 us
  waiting for transfers between devices  464 us (71%)
  local copies, waits for them, and re-layouts  117 us (18%)
  blocking collectives  30.6 us (5%)
  starting transfers between devices  15.2 us (2%)
  between operations  14.1 us (2%)
  matrix products  10.5 us (2%)
    ppermute x16, waiting for transfers between devices, from_behind(): lax.ppermute(shard, axis, [(i, (i + by) % count) for i in range(count)])  212 us
    psum x1, waiting for transfers between devices, body(): summed_band, summed_diagonal = lax.psum((partials, diagonal_part), 'col')  211 us
    dynamic_update_slice x32, local copies, waits for them, and re-layouts, store_block(): lax.dynamic_update_slice(partials, gram_block[:, None, :], (anchor_index,...  116 us
    all_gather x1, waiting for transfers between devices, body(): cotangent_all = lax.all_gather(cotangent, 'row', axis=0, tiled=True)  39.7 us
    all_gather x1, blocking collectives, body(): columns = lax.all_gather(activations, 'col', axis=0, tiled=True)  30.6 us
    ppermute x16, starting transfers between devices, from_behind(): lax.ppermute(shard, axis, [(i, (i + by) % count) for i in range(count)])  15.1 us
  transfers between devices with their start and end apart: 18, of which 18 were waited for; matrix products, arithmetic and copies ran while one was open for 0% of the time, Pallas kernels for 0%

commit v1 on v0

v1 whole, which is shorter than its diff:
```python
import jax
import jax.numpy as jnp
from jax import lax
from jax.experimental import pallas as pl
from jax.experimental.pallas import tpu as pltpu
from jax.sharding import PartitionSpec as P

MESH = pl.DeviceIdType.MESH
DECAY = 0.95
CHUNKS = 4

A0, AM1, AP1, AM2, AP2, XP, XM, XX, STAGE = range(9)
PLACE = {A0: (0, 0), AM1: (-1, 0), AP1: (1, 0), AM2: (-2, 0), AP2: (2, 0), XP: (2, 1), XM: (2, -1), XX: (2, 2)}
TASKS = (
    (A0, A0),
    (A0, AM1), (AP1, AM1),
    (AP1, AM2), (AP2, AM2),
    (XP, AP2), (XP, AP1), (XP, A0), (XP, AM1), (XP, AM2), (XM, AP1), (XM, A0), (XM, AM1),
    (XX, AP1), (XX, A0), (XX, AM1), (XX, None),
)
PHASES = (0, 1, 3, 5, 13, 17)
N = len(TASKS)


def pick(index, values):
    result = jnp.int32(values[0])
    for i, value in enumerate(values):
        if i and value != values[0]:
            result = jnp.where(index == i, jnp.int32(value), result)
    return result


def kernel(
    act_ref, cot_ref, acc_ref, band_ref, diag_ref, band_out, diag_out,
    act_all, cot_all, pan, prod, core_in, half, y_in, piece, fin, fin_diag,
    act_s, act_r, cz_s, cz_r, cx_s, cx_r, cc_s, cc_r, sw_s, sw_r, pan_s, pan_r,
    core_s, core_r, y_s, y_r, fin_s, fin_r, find_r,
):
    row = lax.axis_index("row")
    col = lax.axis_index("col")
    z, xl, co = row // 4, lax.rem(row // 2, 2), lax.rem(row, 2)
    y, xh = col // 2, lax.rem(col, 2)
    x = 2 * xh + xl

    def at(row_, col_):
        return {"row": row_, "col": col_}

    def dev(dz, dx, dy, core):
        zz, xx, yy = lax.rem(z + dz + 8, 8), lax.rem(x + dx + 4, 4), lax.rem(y + dy + 4, 4)
        return at(4 * zz + 2 * lax.rem(xx, 2) + core, 2 * yy + xx // 2)

    def send(src, dst, s_sem, r_sem, device):
        return pltpu.make_async_remote_copy(
            src_ref=src, dst_ref=dst, send_sem=s_sem, recv_sem=r_sem, device_id=device, device_id_type=MESH
        )

    def arrived(dst, sem):
        pltpu.make_async_copy(dst, dst, sem).wait()

    sent = []

    def start(*args):
        copy = send(*args)
        copy.start()
        sent.append(copy)

    z_peers = [at(lax.rem(row + 4 * k, 32), col) for k in range(1, 8)]
    col_peers = [at(row, lax.rem(col + k, 8)) for k in range(1, 8)]
    core_row = row + 1 - 2 * co
    xl_row = row + 2 - 4 * xl
    other_col = col + 1 - 2 * xh
    barrier = pltpu.get_barrier_semaphore()
    greet = z_peers + col_peers + [at(core_row, col), at(xl_row, col), at(xl_row, other_col), at(core_row, other_col)]
    for peer in greet:
        pl.semaphore_signal(barrier, inc=1, device_id=peer, device_id_type=MESH)
    pl.semaphore_wait(barrier, len(greet))

    def cot_piece(row_):
        return cot_all.at[pl.ds(pl.multiple_of(16 * row_, 16), 16)]

    def act_piece(col_):
        return act_all.at[pl.ds(pl.multiple_of(64 * col_, 64), 64)]

    order = (1, 7, 2, 6, 3, 5, 4)
    for k in order:
        start(cot_ref, cot_piece(row), cz_s.at[k], cz_r.at[k], at(lax.rem(row + 4 * k, 32), col))
    start(cot_ref, cot_piece(row), cx_s.at[0], cx_r.at[0], at(xl_row, col))
    start(cot_ref, cot_piece(row), cc_s.at[0], cc_r.at[0], at(core_row, col))
    for k in range(1, 8):
        start(act_ref, act_piece(col), act_s.at[k], act_r.at[k], at(row, lax.rem(col + k, 8)))
    cot_piece(row)[...] = cot_ref[...]
    act_piece(col)[...] = act_ref[...]
    for k in order:
        source = lax.rem(row - 4 * k + 32, 32)
        arrived(cot_piece(source), cz_r.at[k])
        start(cot_piece(source), cot_piece(source), cx_s.at[k], cx_r.at[k], at(xl_row, col))
        start(cot_piece(source), cot_piece(source), cc_s.at[k], cc_r.at[k], at(core_row, col))
    for k in (0,) + order:
        source = lax.rem(xl_row - 4 * k + 32, 32)
        arrived(cot_piece(source), cx_r.at[k])
        start(cot_piece(source), cot_piece(source), cc_s.at[8 + k], cc_r.at[8 + k], at(core_row, col))
    for k in range(1, 8):
        source = lax.rem(col - k + 8, 8)
        arrived(act_piece(source), act_r.at[k])
    for k in (0,) + order:
        source = lax.rem(core_row - 4 * k + 32, 32)
        arrived(cot_piece(source), cc_r.at[k])
    for k in (0,) + order:
        source = lax.rem(core_row + 2 - 4 * xl - 4 * k + 32, 32)
        arrived(cot_piece(source), cc_r.at[8 + k])

    same = xh == co
    own = jnp.where(same, A0, STAGE)
    size = 256 // CHUNKS

    def chunk(slot, i):
        return pan.at[slot, pl.ds(size * i, size)]

    def swap(i):
        return send(chunk(STAGE, i), chunk(A0, i), sw_s.at[i], sw_r.at[i], at(4 * z + 2 * xl + xh, 2 * y + co))

    tall = 128
    for j in range(256 // tall):
        left = act_all[:, tall * j : tall * (j + 1)].T
        rows = pl.ds(tall * j, tall)

        @pl.loop(0, 7)
        def _(n):
            columns = pl.ds(pl.multiple_of(256 * n, 256), 256)
            product = jnp.dot(left, cot_all[:, columns], preferred_element_type=jnp.float32)
            pan[own, rows, columns] = (product + acc_ref[rows, columns].astype(jnp.float32)).astype(jnp.bfloat16)

        per = CHUNKS * tall // 256

        @pl.when(jnp.logical_not(same))
        def _():
            for i in range(per * j, per * (j + 1)):
                swap(i).start()

    def over_z(i, source, up, down):
        start(chunk(source[0], i), chunk(up, i), pan_s.at[up, i], pan_r.at[up, i], dev(1, 0, 0, co))
        start(chunk(source[1], i), chunk(down, i), pan_s.at[down, i], pan_r.at[down, i], dev(-1, 0, 0, co))

    for i in range(CHUNKS):

        @pl.when(jnp.logical_not(same))
        def _():
            arrived(chunk(A0, i), sw_r.at[i])

        over_z(i, (A0, A0), AM1, AP1)

    perm = lambda xx: 2 * lax.rem(xx, 2) + xx // 2
    z_of = [PLACE[a][0] for a in range(8)]
    x_of = [PLACE[a][1] for a in range(8)]

    def rank(slot):
        zz = lax.rem(z + pick(slot, z_of) + 8, 8)
        xx = lax.rem(x + pick(slot, x_of) + 4, 4)
        return 4 * zz + perm(xx)

    def task(t):
        first = pick(t, [a for a, _ in TASKS])
        second = pick(t, [AP2 if b is None else b for _, b in TASKS])
        second = jnp.where((t == N - 1) & (x >= 2), AM2, second)
        ahead = lax.rem(rank(first) - rank(second) + 32, 32)
        swapped = ahead > 16
        left = jnp.where(swapped, second, first)
        right = jnp.where(swapped, first, second)
        return left, right, jnp.where(swapped, 32 - ahead, ahead)

    def core_copy(t):
        theirs = pl.ds(pl.multiple_of(128 * (1 - co), 128), 128)
        return send(prod.at[t, theirs], core_in.at[t], core_s.at[t], core_r.at[t], at(core_row, col))

    def compute(t):
        left, right, _ = task(t)
        prod[t] = lax.dot_general(
            pan[left], pan[right], (((1,), (1,)), ((), ())), preferred_element_type=jnp.float32
        )

    def y_copy(t, k):
        to = lax.rem(y + k, 4)
        rows = pl.ds(pl.multiple_of(32 * to, 32), 32)
        return send(half.at[t, rows], y_in.at[t, k - 1], y_s.at[t, k - 1], y_r.at[t, k - 1], dev(0, 0, k, co))

    def add_cores(t):
        arrived(core_in.at[t], core_r.at[t])
        half[t] = prod[t, pl.ds(pl.multiple_of(128 * co, 128), 128)] + core_in[t]
        for k in (2, 1, 3):
            y_copy(t, k).start()

    part = 4 * co + y
    rows_of_part = pl.ds(pl.multiple_of(32 * part, 32), 32)

    def target(t):
        left, _, ahead = task(t)
        to_row = rank(left)
        to_col = jnp.where(ahead == 0, part, (ahead - 1) // 2)
        return to_row, to_col, lax.rem(ahead + 1, 2), (to_row == row) & (to_col == col)

    def add_y(t, diagonal):
        for k in range(3):
            arrived(y_in.at[t, k], y_r.at[t, k])
        mine = half[t, pl.ds(pl.multiple_of(32 * y, 32), 32)]
        piece[t] = (mine + y_in[t, 1]) + (y_in[t, 0] + y_in[t, 2])
        to_row, to_col, slot, here = target(t)
        dst = fin_diag if diagonal else fin.at[slot, rows_of_part]
        r_sem = find_r.at[0] if diagonal else fin_r.at[slot, part]

        @pl.when(here)
        def _():
            pltpu.make_async_copy(piece.at[t], dst, r_sem).start()

        @pl.when(jnp.logical_not(here))
        def _():
            send(piece.at[t], dst, fin_s.at[t], r_sem, at(to_row, to_col)).start()

    def run(phase):
        @pl.loop(PHASES[phase], PHASES[phase + 1])
        def _(t):
            compute(t)
            core_copy(t).start()

    def reduce_cores(first, last):
        @pl.loop(first, last)
        def _(t):
            add_cores(t)

    def reduce_y(first, last):
        @pl.loop(first, last)
        def _(t):
            add_y(t, False)

    run(0)
    for i in range(CHUNKS):
        arrived(chunk(AM1, i), pan_r.at[AM1, i])
        arrived(chunk(AP1, i), pan_r.at[AP1, i])
        over_z(i, (AM1, AP1), AM2, AP2)
        if i == 0:
            add_cores(0)
        if i == 1:
            add_y(0, True)
    run(1)

    def last_panel(i):
        if i % 2:
            source, device = XM, dev(0, 1, 0, co)
        else:
            source, device = XP, dev(0, -1, 0, co)
        for slot in (XP, XM):
            arrived(chunk(slot, i), pan_r.at[slot, i])
        start(chunk(source, i), chunk(XX, i), pan_s.at[XX, i], pan_r.at[XX, i], device)

    for i in range(CHUNKS):
        arrived(chunk(AP2, i), pan_r.at[AP2, i])
        start(chunk(AP2, i), chunk(XP, i), pan_s.at[XP, i], pan_r.at[XP, i], dev(0, -1, 0, co))
        start(chunk(AP2, i), chunk(XM, i), pan_s.at[XM, i], pan_r.at[XM, i], dev(0, 1, 0, co))
        if i == 0:
            reduce_cores(1, 3)
        if i == 1:
            reduce_y(1, 3)
        if i >= 1:
            last_panel(i - 1)
    for i in range(CHUNKS):
        arrived(chunk(AM2, i), pan_r.at[AM2, i])
    run(2)
    reduce_cores(3, 5)
    last_panel(CHUNKS - 1)
    run(3)
    reduce_cores(5, 13)
    reduce_y(3, 9)
    for i in range(CHUNKS):
        arrived(chunk(XX, i), pan_r.at[XX, i])
    run(4)
    reduce_cores(13, 17)
    reduce_y(9, 17)

    arrived(fin_diag, find_r.at[0])
    diag_out[...] = DECAY * diag_ref[...] + (1.0 - DECAY) * fin_diag[...]
    for slot in range(2):
        for k in range(8):
            arrived(fin.at[slot, pl.ds(32 * k, 32)], fin_r.at[slot, k])
        band_out[:, slot, :] = DECAY * band_ref[:, slot, :] + (1.0 - DECAY) * fin[slot]

    for copy in sent:
        copy.wait_send()

    @pl.when(jnp.logical_not(same))
    def _():
        for i in range(CHUNKS):
            swap(i).wait_send()

    @pl.loop(0, N)
    def _(t):
        core_copy(t).wait_send()
        for k in range(1, 4):
            y_copy(t, k).wait_send()
        to_row, to_col, slot, here = target(t)

        @pl.when(jnp.logical_not(here))
        def _():
            send(piece.at[t], fin_diag, fin_s.at[t], find_r.at[0], at(to_row, to_col)).wait_send()


def body(activations, cotangent, accumulated, band_old, diagonal_old):
    dma = pltpu.SemaphoreType.DMA
    f32, bf16 = jnp.float32, jnp.bfloat16
    vmem = pl.BlockSpec(memory_space=pltpu.VMEM)
    return pl.pallas_call(
        kernel,
        out_shape=(
            jax.ShapeDtypeStruct(band_old.shape, f32),
            jax.ShapeDtypeStruct(diagonal_old.shape, f32),
        ),
        in_specs=[vmem] * 5,
        out_specs=(vmem, vmem),
        scratch_shapes=[
            pltpu.VMEM((512, 256), bf16),
            pltpu.VMEM((512, 1792), bf16),
            pltpu.VMEM((9, 256, 1792), bf16),
            pltpu.VMEM((N, 256, 256), f32),
            pltpu.VMEM((N, 128, 256), f32),
            pltpu.VMEM((N, 128, 256), f32),
            pltpu.VMEM((N, 3, 32, 256), f32),
            pltpu.VMEM((N, 32, 256), f32),
            pltpu.VMEM((2, 256, 256), f32),
            pltpu.VMEM((32, 256), f32),
            dma((8,)), dma((8,)), dma((8,)), dma((8,)), dma((8,)), dma((8,)), dma((16,)), dma((16,)),
            dma((CHUNKS,)), dma((CHUNKS,)), dma((8, CHUNKS)), dma((8, CHUNKS)),
            dma((N,)), dma((N,)), dma((N, 3)), dma((N, 3)), dma((N,)), dma((2, 8)), dma((1,)),
        ],
        compiler_params=pltpu.CompilerParams(
            collective_id=0, has_side_effects=True, vmem_limit_bytes=56 * 2**20
        ),
    )(activations, cotangent, accumulated, band_old, diagonal_old)


def solution(mesh):
    in_specs = (
        P("col", "row"),
        P("row", "col"),
        P("row", "col"),
        P("row", "col", None),
        P(("row", "col"), None),
    )
    out_specs = (P("row", "col", None), P(("row", "col"), None))
    return jax.shard_map(body, mesh=mesh, in_specs=in_specs, out_specs=out_specs, check_vma=False)
```

time: 658 us -> 130 us (0.20)
  waiting for transfers between devices: 464 us -> 0 us
  Pallas kernels: 0 us -> 125 us
  local copies, waits for them, and re-layouts: 117 us -> 2.64 us
  blocking collectives: 30.6 us -> 0 us
  starting transfers between devices: 15.2 us -> 0 us
  between operations: 14.1 us -> 0.65 us
  matrix products: 10.5 us -> 0 us
    ppermute x16 -> x0, waiting for transfers between devices: 212 us -> none  [from_behind(): lax.ppermute(shard, axis, [(i, (i + by) % count) for i in range(count)])]
    psum x1 -> x0, waiting for transfers between devices: 211 us -> none  [body(): summed_band, summed_diagonal = lax.psum((partials, diagonal_part), 'col')]
    pallas_call x0 -> x1, Pallas kernels: none -> 125 us  [body(): pl.pallas_call(kernel, out_shape=(jax.ShapeDtypeStruct(band_old.shape, f3...]
    dynamic_update_slice x32 -> x0, local copies, waits for them, and re-layouts: 116 us -> none  [store_block(): lax.dynamic_update_slice(partials, gram_block[:, None, :], (anchor_index,...]
    all_gather x1 -> x0, waiting for transfers between devices: 39.7 us -> none  [body(): cotangent_all = lax.all_gather(cotangent, 'row', axis=0, tiled=True)]
    all_gather x1 -> x0, blocking collectives: 30.6 us -> none  [body(): columns = lax.all_gather(activations, 'col', axis=0, tiled=True)]
    ppermute x16 -> x0, starting transfers between devices: 15.1 us -> none  [from_behind(): lax.ppermute(shard, axis, [(i, (i + by) % count) for i in range(count)])]
    dot_general x18 -> x0, matrix products: 10.5 us -> none  [the longest x17 8.06 us: block_product(): lax.dot_general(left, right, (((1,), (1,)), ((), ())), preferred_element_...]
  transfers between devices with their start and end apart: 18 -> 0, of which waited for: 18 -> 0; matrix products, arithmetic and copies ran while one was open for 0% -> 0% of each run, Pallas kernels for 0% -> 0%
where the time goes in v1:
time: 130 us; the launch traced here: 129 us
  Pallas kernels  125 us (96%)
  local copies, waits for them, and re-layouts  2.64 us (2%)
    pallas_call x1, Pallas kernels, body(): pl.pallas_call(kernel, out_shape=(jax.ShapeDtypeStruct(band_old.shape, f3...  125 us
    unnamed x4, local copies, waits for them, and re-layouts  2.64 us

profile of v1, /device:TPU:1, one launch (start us, length us, event | category | flops | bytes accessed | tf_op | source)
XLA Modules:
  0.0 128.6 jit_solution(14664022739766264937)
XLA Ops:
  0.6 125.3 %shard_map.68 = (f32[256,2,256]{2,1,0:T(2,128)}, f32[32,256]{1,0:T(8,128)}) custom-call(bf16[64,256]{1,0:T(8,128)(2,1)} %act_ref.1, bf16[16,1792]{1,0:T(8,128)(2,1)} %cot_ref.1, bf16[256,1792]{1,0:T(8,128)(2,1)} %acc_ref.1, f32[256,2,256]{2,1,0:T(2,128)} %band_ref.1, f32[32,256]{1,0:T(8,128)} %diag_ref.1), custom_call_target="tpu_custom_call" | custom-call | tf_op jit(solution)/shard_map/pallas_call | solution.py:309
  125.9 0.0 copy-start
  125.9 2.0 %copy.9 = f32[256,2,256]{2,1,0:T(2,128)} copy(f32[256,2,256]{2,1,0:T(2,128)} %get-tuple-element.4) | data formatting | bytes 1048576
  128.0 0.0 copy-done
  128.0 0.6 copy.10
Async XLA Ops:
  125.9 2.0 %copy-start = (f32[32,256]{1,0:T(8,128)S(1)}, f32[32,256]{1,0:T(8,128)}, u32[]{:S(2)}) copy-start(f32[32,256]{1,0:T(8,128)} %get-tuple-element.5) | copy-start | bytes 98308

commit v2 on v1

v2 whole, which is shorter than its diff:
```python
import jax
import jax.numpy as jnp
from jax import lax
from jax.experimental import pallas as pl
from jax.experimental.pallas import tpu as pltpu
from jax.sharding import PartitionSpec as P

MESH = pl.DeviceIdType.MESH
DECAY = 0.95
CHUNKS = 8
GROUPS = 2
LEAD = 4

A0, AM1, AP1, AM2, AP2, XP, XM, XX, STAGE = range(9)
PLACE = ((0, 0), (-1, 0), (1, 0), (-2, 0), (2, 0), (-2, 1), (-2, -1), (-2, 2))
TASKS = (
    (A0, A0), (A0, AM1), (AP1, AM1),
    (AP1, AM2), (AP1, XP), (A0, XP), (AM1, XP), (AP1, XM), (A0, XM), (AM1, XM),
    (AP1, XX), (A0, XX), (AM1, XX),
    (AP2, AM2), (None, XP), (None, XM), (None, XX),
)
N = len(TASKS)
UNITS = (
    ((0, 1, None), (1, 2, None))
    + tuple((3, 7, g) for g in range(GROUPS))
    + tuple((10, 3, g) for g in range(GROUPS))
    + ((13, 3, None), (16, 1, None))
)


def pick(index, values):
    result = jnp.int32(values[0])
    for i, value in enumerate(values):
        if i and value != values[0]:
            result = jnp.where(index == i, jnp.int32(value), result)
    return result


def kernel(
    act_ref, cot_ref, acc_ref, band_ref, diag_ref, band_out, diag_out,
    act_all, act_t, cot_all, pan, prod, core_in, half, y_in, piece, fin, fin_diag,
    act_s, act_r, cz_s, cz_r, cx_s, cx_r, cc_s, cc_r, sw_s, sw_r, pan_s, pan_r,
    core_s, core_r, y_s, y_r, fin_s, fin_r, find_s, find_r,
):
    row = lax.axis_index("row")
    col = lax.axis_index("col")
    z, xl, co = row // 4, lax.rem(row // 2, 2), lax.rem(row, 2)
    y, xh = col // 2, lax.rem(col, 2)
    x = 2 * xh + xl

    def at(row_, col_):
        return {"row": row_, "col": col_}

    def dev(dz, dx, dy, core):
        zz, xx, yy = lax.rem(z + dz + 8, 8), lax.rem(x + dx + 4, 4), lax.rem(y + dy + 4, 4)
        return at(4 * zz + 2 * lax.rem(xx, 2) + core, 2 * yy + xx // 2)

    def send(src, dst, s_sem, r_sem, device):
        return pltpu.make_async_remote_copy(
            src_ref=src, dst_ref=dst, send_sem=s_sem, recv_sem=r_sem, device_id=device, device_id_type=MESH
        )

    def arrived(dst, sem):
        pltpu.make_async_copy(dst, dst, sem).wait()

    sent = []

    def start(*args):
        copy = send(*args)
        copy.start()
        sent.append(copy)

    up, down = at(lax.rem(row + 4, 32), col), at(lax.rem(row + 28, 32), col)
    col_peers = [at(row, lax.rem(col + k, 8)) for k in range(1, 8)]
    core_row = row + 1 - 2 * co
    xl_row = row + 2 - 4 * xl
    other_col = col + 1 - 2 * xh
    barrier = pltpu.get_barrier_semaphore()
    greet = [up, down] + col_peers + [at(core_row, col), at(xl_row, col), at(xl_row, other_col), at(core_row, other_col)]
    for peer in greet:
        pl.semaphore_signal(barrier, inc=1, device_id=peer, device_id_type=MESH)
    pl.semaphore_wait(barrier, len(greet))

    def cot_piece(row_):
        return cot_all.at[pl.ds(pl.multiple_of(16 * row_, 16), 16)]

    def act_piece(col_):
        return act_all.at[pl.ds(pl.multiple_of(64 * col_, 64), 64)]

    order = (1, 7, 2, 6, 3, 5, 4)
    start(cot_ref, cot_piece(row), cz_s.at[1], cz_r.at[1], up)
    start(cot_ref, cot_piece(row), cz_s.at[7], cz_r.at[7], down)
    start(cot_ref, cot_piece(row), cx_s.at[0], cx_r.at[0], at(xl_row, col))
    start(cot_ref, cot_piece(row), cc_s.at[0], cc_r.at[0], at(core_row, col))
    for k in range(1, 8):
        start(act_ref, act_piece(col), act_s.at[k], act_r.at[k], at(row, lax.rem(col + k, 8)))
    cot_piece(row)[...] = cot_ref[...]
    act_piece(col)[...] = act_ref[...]

    def over_core(rows_of, k, slot, sems):
        source = lax.rem(rows_of - 4 * k + 32, 32)
        arrived(cot_piece(source), sems.at[k])
        start(cot_piece(source), cot_piece(source), cc_s.at[slot], cc_r.at[slot], at(core_row, col))

    for n, k in enumerate(order):
        source = lax.rem(row - 4 * k + 32, 32)
        arrived(cot_piece(source), cz_r.at[k])
        if k < 4:
            start(cot_piece(source), cot_piece(source), cz_s.at[k + 1], cz_r.at[k + 1], up)
        if k > 5:
            start(cot_piece(source), cot_piece(source), cz_s.at[k - 1], cz_r.at[k - 1], down)
        start(cot_piece(source), cot_piece(source), cx_s.at[k], cx_r.at[k], at(xl_row, col))
        start(cot_piece(source), cot_piece(source), cc_s.at[k], cc_r.at[k], at(core_row, col))
        if n == 2:
            for m in range(1, 8):
                arrived(act_piece(lax.rem(col - m + 8, 8)), act_r.at[m])
            act_t[...] = act_all[...].T
        if n > 2:
            over_core(xl_row, ((0,) + order)[n - 3], 8 + ((0,) + order)[n - 3], cx_r)
    for k in order[3:]:
        over_core(xl_row, k, 8 + k, cx_r)
    for k in (0,) + order:
        arrived(cot_piece(lax.rem(core_row - 4 * k + 32, 32)), cc_r.at[k])
    for k in (0,) + order:
        arrived(cot_piece(lax.rem(core_row + 2 - 4 * xl - 4 * k + 32, 32)), cc_r.at[8 + k])

    same = xh == co
    own = jnp.where(same, A0, STAGE)
    size = 256 // CHUNKS

    def chunk(slot, i):
        return pan.at[slot, pl.ds(size * i, size)]

    def swap(i):
        return send(chunk(STAGE, i), chunk(A0, i), sw_s.at[i], sw_r.at[i], at(4 * z + 2 * xl + xh, 2 * y + co))

    def go_up(i, source, to):
        return send(chunk(source, i), chunk(to, i), pan_s.at[to, i], pan_r.at[to, i], up)

    def go_down(i, source, to):
        return send(chunk(source, i), chunk(to, i), pan_s.at[to, i], pan_r.at[to, i], down)

    def own_over_z(i):
        if i < LEAD:
            go_up(i, A0, AM1).start()
        go_down(i, A0, AP1).start()

    tall = 128
    per = CHUNKS * tall // 256
    for j in range(256 // tall):
        rows = pl.ds(tall * j, tall)

        @pl.loop(0, 7)
        def _(n):
            columns = pl.ds(pl.multiple_of(256 * n, 256), 256)
            product = jnp.dot(act_t[rows, :], cot_all[:, columns], preferred_element_type=jnp.float32)
            pan[own, rows, columns] = (product + acc_ref[rows, columns].astype(jnp.float32)).astype(jnp.bfloat16)

        @pl.when(jnp.logical_not(same))
        def _():
            for i in range(per * j, per * (j + 1)):
                swap(i).start()

        @pl.when(same)
        def _():
            for i in range(per * j, per * (j + 1)):
                own_over_z(i)

    @pl.when(jnp.logical_not(same))
    def _():
        for i in range(CHUNKS):
            arrived(chunk(A0, i), sw_r.at[i])
            own_over_z(i)

    for i in range(CHUNKS):
        sent.extend((go_up(i, A0, AM1), go_down(i, A0, AP1)))

    firsts = [AP2 if a is None else a for a, _ in TASKS]
    seconds = [b for _, b in TASKS]

    def rank_of(dz, dx):
        zz, xx = lax.rem(z + dz + 8, 8), lax.rem(x + dx + 4, 4)
        return 4 * zz + 2 * lax.rem(xx, 2) + xx // 2

    ranks = [rank_of(*place) for place in PLACE]

    def either(t):
        return xh == 1 if t == 16 else xl == 1

    def block_of(t):
        first, second = TASKS[t]
        left = ranks[AP2] if first is None else ranks[first]
        right = ranks[second]
        if first is None:
            left = jnp.where(either(t), ranks[AM2], left)
        if t == 13:
            left, right = jnp.where(xl == 1, right, left), jnp.where(xl == 1, left, right)
        ahead = lax.rem(left - right + 32, 32)
        to_col = (ahead - 1) // 2
        return left, to_col, lax.rem(ahead + 1, 2)

    blocks = [None] + [block_of(t) for t in range(1, N)]

    def task(t):
        other = ((t >= 13) & (t <= 15)) & (xl == 1) | (t == 16) & (xh == 1)
        left = jnp.where(other, AM2, pick(t, firsts))
        return left, jnp.where((t == 13) & (xl == 1), AP2, pick(t, seconds))

    def span(u):
        t, n, g = UNITS[u]
        return pl.ds(t, n), pl.ds(0, GROUPS) if g is None else pl.ds(g, 1)

    def core_copy(u):
        tasks, groups = span(u)
        return send(
            prod.at[tasks, groups, pl.ds(pl.multiple_of(128 * (1 - co), 128), 128)], core_in.at[tasks, groups],
            core_s.at[u], core_r.at[u], at(core_row, col),
        )

    def compute(u):
        first_task, count, g = UNITS[u]

        @pl.loop(first_task, first_task + count)
        def _(t):
            left, right = task(t)
            dims = (((1,), (1,)), ((), ()))
            if g is None:
                block = lax.dot_general(pan[left], pan[right], dims, preferred_element_type=jnp.float32)
                prod[t, 0] = block[:, :128]
                prod[t, 1] = block[:, 128:]
            else:
                columns = pan[right, pl.ds(128 * g, 128)]
                prod[t, g] = lax.dot_general(pan[left], columns, dims, preferred_element_type=jnp.float32)

        start_again(core_copy(u))

    def start_again(copy):
        copy.start()
        sent.append(copy)

    def add_cores(u):
        tasks, groups = span(u)
        arrived(core_in.at[tasks, groups], core_r.at[u])
        half[tasks, groups] = prod[tasks, groups, pl.ds(pl.multiple_of(128 * co, 128), 128)] + core_in[tasks, groups]
        for k in (2, 1, 3):
            to = lax.rem(y + k, 4)
            start_again(send(
                half.at[tasks, groups, pl.ds(pl.multiple_of(32 * to, 32), 32)], y_in.at[k - 1, tasks, groups],
                y_s.at[u, k - 1], y_r.at[u, k - 1], dev(0, 0, k, co),
            ))

    part = 4 * co + y
    rows_of_part = pl.ds(pl.multiple_of(32 * part, 32), 32)

    def deliver(src, dst, s_sem, r_sem, to_row, to_col, begin):
        here = (to_row == row) & (to_col == col)
        if begin:

            @pl.when(here)
            def _():
                pltpu.make_async_copy(src, dst, r_sem).start()

        @pl.when(jnp.logical_not(here))
        def _():
            copy = send(src, dst, s_sem, r_sem, at(to_row, to_col))
            if begin:
                copy.start()
            else:
                copy.wait_send()

    def deliver_diagonal(begin):
        deliver(piece.at[0], fin_diag, find_s.at[0], find_r.at[0], ranks[A0], part, begin)

    def deliver_block(t, g, begin):
        to_row, to_col, slot = blocks[t]
        deliver(
            piece.at[t, g], fin.at[slot, g, rows_of_part], fin_s.at[t, g], fin_r.at[slot, g, part],
            to_row, to_col, begin,
        )

    def add_y(u):
        tasks, groups = span(u)
        for k in range(3):
            arrived(y_in.at[k, tasks, groups], y_r.at[u, k])
        mine = half[tasks, groups, pl.ds(pl.multiple_of(32 * y, 32), 32)]
        piece[tasks, groups] = (mine + y_in[1, tasks, groups]) + (y_in[0, tasks, groups] + y_in[2, tasks, groups])

    def finish(u):
        first_task, count, group = UNITS[u]

        for t in range(first_task, first_task + count):
            for g in range(GROUPS):
                if group is None or group == g:
                    deliver_block(t, g, True)

    def last_panel(i):
        for slot in (XP, XM):
            arrived(chunk(slot, i), pan_r.at[slot, i])
        source, device = (XM, dev(0, 1, 0, co)) if i % 2 else (XP, dev(0, -1, 0, co))
        start(chunk(source, i), chunk(XX, i), pan_s.at[XX, i], pan_r.at[XX, i], device)

    def last_arrived(i):
        arrived(chunk(XX, i), pan_r.at[XX, i])

    def arm(k):
        arrived(chunk(AM2, k), pan_r.at[AM2, k])
        start(chunk(AM2, k), chunk(XP, k), pan_s.at[XP, k], pan_r.at[XP, k], dev(0, -1, 0, co))
        start(chunk(AM2, k), chunk(XM, k), pan_s.at[XM, k], pan_r.at[XM, k], dev(0, 1, 0, co))
        if k >= 1:
            last_panel(k - 1)

    compute(0)
    for i in range(CHUNKS):
        if i >= LEAD:
            arm(i - LEAD)
        arrived(chunk(AM1, i), pan_r.at[AM1, i])
        start_again(go_up(i, AM1, AM2))
        if i + LEAD < CHUNKS:
            go_up(i + LEAD, A0, AM1).start()
        arrived(chunk(AP1, i), pan_r.at[AP1, i])
        start_again(go_down(i, AP1, AP2))
        if i == 1:
            add_cores(0)
        if i == 4:
            add_y(0)
            deliver_diagonal(True)
    compute(1)
    for k in range(CHUNKS - LEAD, CHUNKS):
        arm(k)
        if k == max(3, CHUNKS - LEAD):
            add_cores(1)
        if k == 4:
            compute(2)
        if k == 5:
            add_cores(2)
            add_y(1)
            finish(1)
            for i in range(4):
                last_arrived(i)
            compute(4)
        if k == 6:
            add_cores(4)
            add_y(2)
            finish(2)
        if k == 7:
            add_y(4)
            finish(4)
    last_panel(CHUNKS - 1)
    compute(3)
    for i in range(CHUNKS):
        arrived(chunk(AP2, i), pan_r.at[AP2, i])
    compute(6)
    add_cores(3)
    for i in range(4, CHUNKS):
        last_arrived(i)
    compute(5)
    compute(7)
    add_cores(6)
    add_y(3)
    finish(3)
    add_cores(5)
    add_cores(7)
    add_y(6)
    finish(6)
    add_y(5)
    finish(5)
    add_y(7)
    finish(7)

    arrived(fin_diag, find_r.at[0])
    for g in range(GROUPS):
        lanes = pl.ds(128 * g, 128)
        diag_out[:, lanes] = DECAY * diag_ref[:, lanes] + (1.0 - DECAY) * fin_diag[g]
    for slot in range(2):
        for k in range(8):
            for g in range(GROUPS):
                arrived(fin.at[slot, g, pl.ds(32 * k, 32)], fin_r.at[slot, g, k])
        for g in range(GROUPS):
            lanes = pl.ds(128 * g, 128)
            band_out[:, slot, lanes] = DECAY * band_ref[:, slot, lanes] + (1.0 - DECAY) * fin[slot, g]

    for copy in sent:
        copy.wait_send()

    @pl.when(jnp.logical_not(same))
    def _():
        for i in range(CHUNKS):
            swap(i).wait_send()

    deliver_diagonal(False)

    for t in range(1, N):
        for g in range(GROUPS):
            deliver_block(t, g, False)


def body(activations, cotangent, accumulated, band_old, diagonal_old):
    dma = pltpu.SemaphoreType.DMA
    f32, bf16 = jnp.float32, jnp.bfloat16
    vmem = pl.BlockSpec(memory_space=pltpu.VMEM)
    return pl.pallas_call(
        kernel,
        out_shape=(
            jax.ShapeDtypeStruct(band_old.shape, f32),
            jax.ShapeDtypeStruct(diagonal_old.shape, f32),
        ),
        in_specs=[vmem] * 5,
        out_specs=(vmem, vmem),
        scratch_shapes=[
            pltpu.VMEM((512, 256), bf16),
            pltpu.VMEM((256, 512), bf16),
            pltpu.VMEM((512, 1792), bf16),
            pltpu.VMEM((9, 256, 1792), bf16),
            pltpu.VMEM((N, GROUPS, 256, 128), f32),
            pltpu.VMEM((N, GROUPS, 128, 128), f32),
            pltpu.VMEM((N, GROUPS, 128, 128), f32),
            pltpu.VMEM((3, N, GROUPS, 32, 128), f32),
            pltpu.VMEM((N, GROUPS, 32, 128), f32),
            pltpu.VMEM((2, GROUPS, 256, 128), f32),
            pltpu.VMEM((GROUPS, 32, 128), f32),
            dma((8,)), dma((8,)), dma((8,)), dma((8,)), dma((8,)), dma((8,)), dma((16,)), dma((16,)),
            dma((CHUNKS,)), dma((CHUNKS,)), dma((8, CHUNKS)), dma((8, CHUNKS)),
            dma((len(UNITS),)), dma((len(UNITS),)), dma((len(UNITS), 3)), dma((len(UNITS), 3)),
            dma((N, GROUPS)), dma((2, GROUPS, 8)), dma((1,)), dma((1,)),
        ],
        compiler_params=pltpu.CompilerParams(
            collective_id=0, has_side_effects=True, vmem_limit_bytes=56 * 2**20
        ),
    )(activations, cotangent, accumulated, band_old, diagonal_old)


def solution(mesh):
    in_specs = (
        P("col", "row"),
        P("row", "col"),
        P("row", "col"),
        P("row", "col", None),
        P(("row", "col"), None),
    )
    out_specs = (P("row", "col", None), P(("row", "col"), None))
    return jax.shard_map(body, mesh=mesh, in_specs=in_specs, out_specs=out_specs, check_vma=False)
```

time: 130 us -> 127 us (0.977); the launches traced: 129 us -> 127 us
    pallas_call x1, Pallas kernels: 125 us -> 124 us  [body(): pl.pallas_call(kernel, out_shape=(jax.ShapeDtypeStruct(band_old.shape, f3...]
where the time goes in v2:
time: 127 us
  Pallas kernels  124 us (98%)
  local copies, waits for them, and re-layouts  2.64 us (2%)
    pallas_call x1, Pallas kernels, body(): pl.pallas_call(kernel, out_shape=(jax.ShapeDtypeStruct(band_old.shape, f3...  124 us
    unnamed x4, local copies, waits for them, and re-layouts  2.64 us

profile of v2, /device:TPU:1, one launch (start us, length us, event | category | flops | bytes accessed | tf_op | source)
XLA Modules:
  0.0 127.2 jit_solution(10037341826730376255)
XLA Ops:
  0.6 123.9 %shard_map.68 = (f32[256,2,256]{2,1,0:T(2,128)}, f32[32,256]{1,0:T(8,128)}) custom-call(bf16[64,256]{1,0:T(8,128)(2,1)} %act_ref.1, bf16[16,1792]{1,0:T(8,128)(2,1)} %cot_ref.1, bf16[256,1792]{1,0:T(8,128)(2,1)} %acc_ref.1, f32[256,2,256]{2,1,0:T(2,128)} %band_ref.1, f32[32,256]{1,0:T(8,128)} %diag_ref.1), custom_call_target="tpu_custom_call" | custom-call | tf_op jit(solution)/shard_map/pallas_call | solution.py:401
  124.6 0.0 copy-start
  124.6 2.0 %copy.9 = f32[256,2,256]{2,1,0:T(2,128)} copy(f32[256,2,256]{2,1,0:T(2,128)} %get-tuple-element.4) | data formatting | bytes 1048576
  126.6 0.0 copy-done
  126.6 0.6 copy.10
Async XLA Ops:
  124.6 2.0 %copy-start = (f32[32,256]{1,0:T(8,128)S(1)}, f32[32,256]{1,0:T(8,128)}, u32[]{:S(2)}) copy-start(f32[32,256]{1,0:T(8,128)} %get-tuple-element.5) | copy-start | bytes 98308

commit v3 on v2

--- a/solution.py
+++ b/solution.py
@@ -21,10 +21,9 @@
 )
 N = len(TASKS)
 UNITS = (
-    ((0, 1, None), (1, 2, None))
-    + tuple((3, 7, g) for g in range(GROUPS))
-    + tuple((10, 3, g) for g in range(GROUPS))
-    + ((13, 3, None), (16, 1, None))
+    (0, 1, None), (1, 2, None),
+    (3, 3, 0), (3, 1, 1), (10, 3, 0), (10, 3, 1),
+    (13, 1, None), (16, 1, 1), (4, 6, 1), (14, 2, 1), (14, 3, 0), (6, 4, 0),
 )
 
 
@@ -72,11 +71,12 @@
 
     up, down = at(lax.rem(row + 4, 32), col), at(lax.rem(row + 28, 32), col)
     col_peers = [at(row, lax.rem(col + k, 8)) for k in range(1, 8)]
+    up_2, down_2 = at(lax.rem(row + 8, 32), col), at(lax.rem(row + 24, 32), col)
     core_row = row + 1 - 2 * co
     xl_row = row + 2 - 4 * xl
     other_col = col + 1 - 2 * xh
     barrier = pltpu.get_barrier_semaphore()
-    greet = [up, down] + col_peers + [at(core_row, col), at(xl_row, col), at(xl_row, other_col), at(core_row, other_col)]
+    greet = [up, down, up_2, down_2] + col_peers + [at(core_row, col), at(xl_row, col), at(xl_row, other_col), at(core_row, other_col)]
     for peer in greet:
         pl.semaphore_signal(barrier, inc=1, device_id=peer, device_id_type=MESH)
     pl.semaphore_wait(barrier, len(greet))
@@ -90,6 +90,8 @@
     order = (1, 7, 2, 6, 3, 5, 4)
     start(cot_ref, cot_piece(row), cz_s.at[1], cz_r.at[1], up)
     start(cot_ref, cot_piece(row), cz_s.at[7], cz_r.at[7], down)
+    start(cot_ref, cot_piece(row), cz_s.at[2], cz_r.at[2], up_2)
+    start(cot_ref, cot_piece(row), cz_s.at[6], cz_r.at[6], down_2)
     start(cot_ref, cot_piece(row), cx_s.at[0], cx_r.at[0], at(xl_row, col))
     start(cot_ref, cot_piece(row), cc_s.at[0], cc_r.at[0], at(core_row, col))
     for k in range(1, 8):
@@ -97,28 +99,27 @@
     cot_piece(row)[...] = cot_ref[...]
     act_piece(col)[...] = act_ref[...]
 
-    def over_core(rows_of, k, slot, sems):
-        source = lax.rem(rows_of - 4 * k + 32, 32)
-        arrived(cot_piece(source), sems.at[k])
-        start(cot_piece(source), cot_piece(source), cc_s.at[slot], cc_r.at[slot], at(core_row, col))
-
-    for n, k in enumerate(order):
-        source = lax.rem(row - 4 * k + 32, 32)
-        arrived(cot_piece(source), cz_r.at[k])
-        if k < 4:
-            start(cot_piece(source), cot_piece(source), cz_s.at[k + 1], cz_r.at[k + 1], up)
-        if k > 5:
-            start(cot_piece(source), cot_piece(source), cz_s.at[k - 1], cz_r.at[k - 1], down)
-        start(cot_piece(source), cot_piece(source), cx_s.at[k], cx_r.at[k], at(xl_row, col))
-        start(cot_piece(source), cot_piece(source), cc_s.at[k], cc_r.at[k], at(core_row, col))
-        if n == 2:
+    onward = {1: (3, up_2), 2: (4, up_2), 7: (5, down_2)}
+
+    def beside(k):
+        piece_in = cot_piece(lax.rem(xl_row - 4 * k + 32, 32))
+        arrived(piece_in, cx_r.at[k])
+        start(piece_in, piece_in, cc_s.at[8 + k], cc_r.at[8 + k], at(core_row, col))
+
+    after = {1: (0,), 7: (), 2: (1,), 6: (7,), 3: (2,), 5: (6,), 4: (3, 5, 4)}
+    for k in order:
+        piece_in = cot_piece(lax.rem(row - 4 * k + 32, 32))
+        arrived(piece_in, cz_r.at[k])
+        if k in onward:
+            start(piece_in, piece_in, cz_s.at[onward[k][0]], cz_r.at[onward[k][0]], onward[k][1])
+        start(piece_in, piece_in, cx_s.at[k], cx_r.at[k], at(xl_row, col))
+        start(piece_in, piece_in, cc_s.at[k], cc_r.at[k], at(core_row, col))
+        for other in after[k]:
+            beside(other)
+        if k == 6:
             for m in range(1, 8):
                 arrived(act_piece(lax.rem(col - m + 8, 8)), act_r.at[m])
             act_t[...] = act_all[...].T
-        if n > 2:
-            over_core(xl_row, ((0,) + order)[n - 3], 8 + ((0,) + order)[n - 3], cx_r)
-    for k in order[3:]:
-        over_core(xl_row, k, 8 + k, cx_r)
     for k in (0,) + order:
         arrived(cot_piece(lax.rem(core_row - 4 * k + 32, 32)), cc_r.at[k])
     for k in (0,) + order:
@@ -327,45 +328,48 @@
     compute(1)
     for k in range(CHUNKS - LEAD, CHUNKS):
         arm(k)
-        if k == max(3, CHUNKS - LEAD):
-            add_cores(1)
         if k == 4:
             compute(2)
+            add_cores(1)
         if k == 5:
+            compute(11)
             add_cores(2)
-            add_y(1)
-            finish(1)
+        if k == 6:
+            add_cores(11)
             for i in range(4):
                 last_arrived(i)
             compute(4)
-        if k == 6:
+            add_y(1)
+            finish(1)
+        if k == 7:
             add_cores(4)
-            add_y(2)
-            finish(2)
-        if k == 7:
-            add_y(4)
-            finish(4)
-    last_panel(CHUNKS - 1)
     compute(3)
     for i in range(CHUNKS):
         arrived(chunk(AP2, i), pan_r.at[AP2, i])
     compute(6)
+    compute(10)
+    last_panel(CHUNKS - 1)
     add_cores(3)
+    add_cores(6)
+    compute(8)
+    add_cores(10)
+    compute(9)
+    add_cores(8)
+    add_cores(9)
+    for u in (2, 11, 4, 3, 6):
+        add_y(u)
+        finish(u)
     for i in range(4, CHUNKS):
         last_arrived(i)
     compute(5)
     compute(7)
-    add_cores(6)
-    add_y(3)
-    finish(3)
+    add_y(10)
+    finish(10)
     add_cores(5)
     add_cores(7)
-    add_y(6)
-    finish(6)
-    add_y(5)
-    finish(5)
-    add_y(7)
-    finish(7)
+    for u in (8, 9, 5, 7):
+        add_y(u)
+        finish(u)
 
     arrived(fin_diag, find_r.at[0])
     for g in range(GROUPS):

time: 127 us -> 118 us (0.929)
  Pallas kernels: 124 us -> 114 us
    pallas_call x1, Pallas kernels: 124 us -> 114 us  [body(): pl.pallas_call(kernel, out_shape=(jax.ShapeDtypeStruct(band_old.shape, f3...]
where the time goes in v3:
time: 118 us; the launch traced here: 117 us
  Pallas kernels  114 us (97%)
  local copies, waits for them, and re-layouts  2.64 us (2%)
    pallas_call x1, Pallas kernels, body(): pl.pallas_call(kernel, out_shape=(jax.ShapeDtypeStruct(band_old.shape, f3...  114 us
    unnamed x4, local copies, waits for them, and re-layouts  2.64 us

profile of v3, /device:TPU:1, one launch (start us, length us, event | category | flops | bytes accessed | tf_op | source)
XLA Modules:
  0.0 117.4 jit_solution(17120378384225554939)
XLA Ops:
  0.6 114.1 %shard_map.68 = (f32[256,2,256]{2,1,0:T(2,128)}, f32[32,256]{1,0:T(8,128)}) custom-call(bf16[64,256]{1,0:T(8,128)(2,1)} %act_ref.1, bf16[16,1792]{1,0:T(8,128)(2,1)} %cot_ref.1, bf16[256,1792]{1,0:T(8,128)(2,1)} %acc_ref.1, f32[256,2,256]{2,1,0:T(2,128)} %band_ref.1, f32[32,256]{1,0:T(8,128)} %diag_ref.1), custom_call_target="tpu_custom_call" | custom-call | tf_op jit(solution)/shard_map/pallas_call | solution.py:405
  114.7 0.0 copy-start
  114.8 2.0 %copy.9 = f32[256,2,256]{2,1,0:T(2,128)} copy(f32[256,2,256]{2,1,0:T(2,128)} %get-tuple-element.4) | data formatting | bytes 1048576
  116.8 0.0 copy-done
  116.8 0.6 copy.10
Async XLA Ops:
  114.7 2.0 %copy-start = (f32[32,256]{1,0:T(8,128)S(1)}, f32[32,256]{1,0:T(8,128)}, u32[]{:S(2)}) copy-start(f32[32,256]{1,0:T(8,128)} %get-tuple-element.5) | copy-start | bytes 98308

commit v4 on v3

--- a/solution.py
+++ b/solution.py
@@ -15,7 +15,7 @@
 PLACE = ((0, 0), (-1, 0), (1, 0), (-2, 0), (2, 0), (-2, 1), (-2, -1), (-2, 2))
 TASKS = (
     (A0, A0), (A0, AM1), (AP1, AM1),
-    (AP1, AM2), (AP1, XP), (A0, XP), (AM1, XP), (AP1, XM), (A0, XM), (AM1, XM),
+    (AP1, AM2), (AP1, XP), (AP1, XM), (A0, XP), (A0, XM), (AM1, XP), (AM1, XM),
     (AP1, XX), (A0, XX), (AM1, XX),
     (AP2, AM2), (None, XP), (None, XM), (None, XX),
 )
@@ -36,7 +36,8 @@
 
 
 def kernel(
-    act_ref, cot_ref, acc_ref, band_ref, diag_ref, band_out, diag_out,
+    act_ref, cot_ref, acc_hbm, band_hbm, diag_ref, band_out, diag_out,
+    acc_ref, band_ref, load_s,
     act_all, act_t, cot_all, pan, prod, core_in, half, y_in, piece, fin, fin_diag,
     act_s, act_r, cz_s, cz_r, cx_s, cx_r, cc_s, cc_r, sw_s, sw_r, pan_s, pan_r,
     core_s, core_r, y_s, y_r, fin_s, fin_r, find_s, find_r,
@@ -75,6 +76,12 @@
     core_row = row + 1 - 2 * co
     xl_row = row + 2 - 4 * xl
     other_col = col + 1 - 2 * xh
+    loads = (
+        pltpu.make_async_copy(acc_hbm, acc_ref, load_s.at[0]),
+        pltpu.make_async_copy(band_hbm, band_ref, load_s.at[1]),
+    )
+    for load in loads:
+        load.start()
     barrier = pltpu.get_barrier_semaphore()
     greet = [up, down, up_2, down_2] + col_peers + [at(core_row, col), at(xl_row, col), at(xl_row, other_col), at(core_row, other_col)]
     for peer in greet:
@@ -130,6 +137,9 @@
     size = 256 // CHUNKS
 
     def chunk(slot, i):
+        if slot in (XP, XM):
+            half_of, first = divmod(size * i, 128)
+            return pan.at[XP + half_of, pl.ds(first + 128 * (slot - XP), size)]
         return pan.at[slot, pl.ds(size * i, size)]
 
     def swap(i):
@@ -146,6 +156,7 @@
             go_up(i, A0, AM1).start()
         go_down(i, A0, AP1).start()
 
+    loads[0].wait()
     tall = 128
     per = CHUNKS * tall // 256
     for j in range(256 // tall):
@@ -218,21 +229,49 @@
             core_s.at[u], core_r.at[u], at(core_row, col),
         )
 
+    def multiply(left, right):
+        return lax.dot_general(
+            pan[left], right, (((1,), (1,)), ((), ())), preferred_element_type=jnp.float32
+        )
+
     def compute(u):
         first_task, count, g = UNITS[u]
-
-        @pl.loop(first_task, first_task + count)
-        def _(t):
-            left, right = task(t)
-            dims = (((1,), (1,)), ((), ()))
-            if g is None:
-                block = lax.dot_general(pan[left], pan[right], dims, preferred_element_type=jnp.float32)
+        if g is None:
+
+            @pl.loop(first_task, first_task + count)
+            def _(t):
+                left, right = task(t)
+                block = multiply(left, pan[right])
                 prod[t, 0] = block[:, :128]
                 prod[t, 1] = block[:, 128:]
-            else:
-                columns = pan[right, pl.ds(128 * g, 128)]
-                prod[t, g] = lax.dot_general(pan[left], columns, dims, preferred_element_type=jnp.float32)
-
+
+        else:
+            t, last = first_task, first_task + count
+            while t < last:
+                if TASKS[t][1] == XP:
+                    pairs = 1
+                    while t + 2 * pairs + 1 < last and TASKS[t + 2 * pairs][1] == XP:
+                        pairs += 1
+
+                    @pl.loop(0, pairs)
+                    def _(n, t=t):
+                        left, _ = task(t + 2 * n)
+                        block = multiply(left, pan[XP + g])
+                        prod[t + 2 * n, g] = block[:, :128]
+                        prod[t + 2 * n + 1, g] = block[:, 128:]
+
+                    t += 2 * pairs
+                else:
+                    others = 1
+                    while t + others < last and TASKS[t + others][1] != XP:
+                        others += 1
+
+                    @pl.loop(t, t + others)
+                    def _(n):
+                        left, right = task(n)
+                        prod[n, g] = multiply(left, pan[right, pl.ds(128 * g, 128)])
+
+                    t += others
         start_again(core_copy(u))
 
     def start_again(copy):
@@ -371,6 +410,7 @@
         add_y(u)
         finish(u)
 
+    loads[1].wait()
     arrived(fin_diag, find_r.at[0])
     for g in range(GROUPS):
         lanes = pl.ds(128 * g, 128)
@@ -402,15 +442,19 @@
     dma = pltpu.SemaphoreType.DMA
     f32, bf16 = jnp.float32, jnp.bfloat16
     vmem = pl.BlockSpec(memory_space=pltpu.VMEM)
+    hbm = pl.BlockSpec(memory_space=pl.ANY)
     return pl.pallas_call(
         kernel,
         out_shape=(
             jax.ShapeDtypeStruct(band_old.shape, f32),
             jax.ShapeDtypeStruct(diagonal_old.shape, f32),
         ),
-        in_specs=[vmem] * 5,
+        in_specs=[vmem, vmem, hbm, hbm, vmem],
         out_specs=(vmem, vmem),
         scratch_shapes=[
+            pltpu.VMEM(accumulated.shape, bf16),
+            pltpu.VMEM(band_old.shape, f32),
+            dma((2,)),
             pltpu.VMEM((512, 256), bf16),
             pltpu.VMEM((256, 512), bf16),
             pltpu.VMEM((512, 1792), bf16),

time: 118 us -> 116 us (0.983)
  Pallas kernels: 114 us -> 112 us
    pallas_call x1, Pallas kernels: 114 us -> 112 us  [body(): pl.pallas_call(kernel, out_shape=(jax.ShapeDtypeStruct(band_old.shape, f3...]
where the time goes in v4:
time: 116 us
  Pallas kernels  112 us (97%)
  local copies, waits for them, and re-layouts  2.64 us (2%)
    pallas_call x1, Pallas kernels, body(): pl.pallas_call(kernel, out_shape=(jax.ShapeDtypeStruct(band_old.shape, f3...  112 us
    unnamed x4, local copies, waits for them, and re-layouts  2.64 us

profile of v4, /device:TPU:1, one launch (start us, length us, event | category | flops | bytes accessed | tf_op | source)
XLA Modules:
  0.0 115.6 jit_solution(17677458452593578205)
XLA Ops:
  0.6 112.3 %shard_map.68 = (f32[256,2,256]{2,1,0:T(2,128)}, f32[32,256]{1,0:T(8,128)}) custom-call(bf16[64,256]{1,0:T(8,128)(2,1)} %act_ref.1, bf16[16,1792]{1,0:T(8,128)(2,1)} %cot_ref.1, bf16[256,1792]{1,0:T(8,128)(2,1)} %acc_hbm.1, f32[256,2,256]{2,1,0:T(2,128)} %band_hbm.1, f32[32,256]{1,0:T(8,128)} %diag_ref.1), custom_call_target="tpu_custom_call" | custom-call | tf_op jit(solution)/shard_map/pallas_call | solution.py:446
  113.0 0.0 copy-start
  113.0 2.0 %copy.9 = f32[256,2,256]{2,1,0:T(2,128)} copy(f32[256,2,256]{2,1,0:T(2,128)} %get-tuple-element.4) | data formatting | bytes 1048576
  115.0 0.0 copy-done
  115.0 0.6 copy.10
Async XLA Ops:
  113.0 2.0 %copy-start = (f32[32,256]{1,0:T(8,128)S(1)}, f32[32,256]{1,0:T(8,128)}, u32[]{:S(2)}) copy-start(f32[32,256]{1,0:T(8,128)} %get-tuple-element.5) | copy-start | bytes 98308

commit v5 on v4

--- a/solution.py
+++ b/solution.py
@@ -123,10 +123,9 @@
         start(piece_in, piece_in, cc_s.at[k], cc_r.at[k], at(core_row, col))
         for other in after[k]:
             beside(other)
-        if k == 6:
-            for m in range(1, 8):
-                arrived(act_piece(lax.rem(col - m + 8, 8)), act_r.at[m])
-            act_t[...] = act_all[...].T
+    for m in range(1, 8):
+        arrived(act_piece(lax.rem(col - m + 8, 8)), act_r.at[m])
+    act_t[...] = act_all[...].T
     for k in (0,) + order:
         arrived(cot_piece(lax.rem(core_row - 4 * k + 32, 32)), cc_r.at[k])
     for k in (0,) + order:
@@ -162,9 +161,8 @@
     for j in range(256 // tall):
         rows = pl.ds(tall * j, tall)
 
-        @pl.loop(0, 7)
-        def _(n):
-            columns = pl.ds(pl.multiple_of(256 * n, 256), 256)
+        for n in range(7):
+            columns = pl.ds(256 * n, 256)
             product = jnp.dot(act_t[rows, :], cot_all[:, columns], preferred_element_type=jnp.float32)
             pan[own, rows, columns] = (product + acc_ref[rows, columns].astype(jnp.float32)).astype(jnp.bfloat16)
 
@@ -364,24 +362,24 @@
         if i == 4:
             add_y(0)
             deliver_diagonal(True)
-    compute(1)
     for k in range(CHUNKS - LEAD, CHUNKS):
         arm(k)
         if k == 4:
+            compute(1)
             compute(2)
-            add_cores(1)
         if k == 5:
             compute(11)
+            add_cores(1)
             add_cores(2)
         if k == 6:
             add_cores(11)
             for i in range(4):
                 last_arrived(i)
             compute(4)
+        if k == 7:
+            add_cores(4)
             add_y(1)
             finish(1)
-        if k == 7:
-            add_cores(4)
     compute(3)
     for i in range(CHUNKS):
         arrived(chunk(AP2, i), pan_r.at[AP2, i])

time: 116 us -> 115 us (level)
  no operation moved by 1% of the time
where the time goes in v5:
time: 115 us
  Pallas kernels  111 us (97%)
  local copies, waits for them, and re-layouts  2.64 us (2%)
    pallas_call x1, Pallas kernels, body(): pl.pallas_call(kernel, out_shape=(jax.ShapeDtypeStruct(band_old.shape, f3...  111 us
    unnamed x4, local copies, waits for them, and re-layouts  2.64 us

profile of v5, /device:TPU:1, one launch (start us, length us, event | category | flops | bytes accessed | tf_op | source)
XLA Modules:
  0.0 114.8 jit_solution(13549437835728840106)
XLA Ops:
  0.6 111.5 %shard_map.68 = (f32[256,2,256]{2,1,0:T(2,128)}, f32[32,256]{1,0:T(8,128)}) custom-call(bf16[64,256]{1,0:T(8,128)(2,1)} %act_ref.1, bf16[16,1792]{1,0:T(8,128)(2,1)} %cot_ref.1, bf16[256,1792]{1,0:T(8,128)(2,1)} %acc_hbm.1, f32[256,2,256]{2,1,0:T(2,128)} %band_hbm.1, f32[32,256]{1,0:T(8,128)} %diag_ref.1), custom_call_target="tpu_custom_call" | custom-call | tf_op jit(solution)/shard_map/pallas_call | solution.py:444
  112.1 0.0 copy-start
  112.1 2.0 %copy.9 = f32[256,2,256]{2,1,0:T(2,128)} copy(f32[256,2,256]{2,1,0:T(2,128)} %get-tuple-element.4) | data formatting | bytes 1048576
  114.2 0.0 copy-done
  114.2 0.6 copy.10
Async XLA Ops:
  112.1 2.0 %copy-start = (f32[32,256]{1,0:T(8,128)S(1)}, f32[32,256]{1,0:T(8,128)}, u32[]{:S(2)}) copy-start(f32[32,256]{1,0:T(8,128)} %get-tuple-element.5) | copy-start | bytes 98308

commit v6 on v5

--- a/solution.py
+++ b/solution.py
@@ -362,24 +362,24 @@
         if i == 4:
             add_y(0)
             deliver_diagonal(True)
+    compute(1)
     for k in range(CHUNKS - LEAD, CHUNKS):
         arm(k)
         if k == 4:
-            compute(1)
             compute(2)
+            add_cores(1)
         if k == 5:
             compute(11)
-            add_cores(1)
             add_cores(2)
         if k == 6:
             add_cores(11)
             for i in range(4):
                 last_arrived(i)
             compute(4)
+            add_y(1)
+            finish(1)
         if k == 7:
             add_cores(4)
-            add_y(1)
-            finish(1)
     compute(3)
     for i in range(CHUNKS):
         arrived(chunk(AP2, i), pan_r.at[AP2, i])
@@ -400,11 +400,9 @@
         last_arrived(i)
     compute(5)
     compute(7)
-    add_y(10)
-    finish(10)
     add_cores(5)
     add_cores(7)
-    for u in (8, 9, 5, 7):
+    for u in (10, 8, 9, 5, 7):
         add_y(u)
         finish(u)
 

time: 115 us -> 115 us (level)
  no operation moved by 1% of the time
where the time goes in v6:
time: 115 us
  Pallas kernels  111 us (97%)
  local copies, waits for them, and re-layouts  2.64 us (2%)
    pallas_call x1, Pallas kernels, body(): pl.pallas_call(kernel, out_shape=(jax.ShapeDtypeStruct(band_old.shape, f3...  111 us
    unnamed x4, local copies, waits for them, and re-layouts  2.64 us

profile of v6, /device:TPU:1, one launch (start us, length us, event | category | flops | bytes accessed | tf_op | source)
XLA Modules:
  0.0 114.7 jit_solution(4654706795908023135)
XLA Ops:
  0.6 111.4 %shard_map.68 = (f32[256,2,256]{2,1,0:T(2,128)}, f32[32,256]{1,0:T(8,128)}) custom-call(bf16[64,256]{1,0:T(8,128)(2,1)} %act_ref.1, bf16[16,1792]{1,0:T(8,128)(2,1)} %cot_ref.1, bf16[256,1792]{1,0:T(8,128)(2,1)} %acc_hbm.1, f32[256,2,256]{2,1,0:T(2,128)} %band_hbm.1, f32[32,256]{1,0:T(8,128)} %diag_ref.1), custom_call_target="tpu_custom_call" | custom-call | tf_op jit(solution)/shard_map/pallas_call | solution.py:442
  112.0 0.0 copy-start
  112.0 2.0 %copy.9 = f32[256,2,256]{2,1,0:T(2,128)} copy(f32[256,2,256]{2,1,0:T(2,128)} %get-tuple-element.4) | data formatting | bytes 1048576
  114.0 0.0 copy-done
  114.0 0.6 copy.10
Async XLA Ops:
  112.0 2.0 %copy-start = (f32[32,256]{1,0:T(8,128)S(1)}, f32[32,256]{1,0:T(8,128)}, u32[]{:S(2)}) copy-start(f32[32,256]{1,0:T(8,128)} %get-tuple-element.5) | copy-start | bytes 98308
